TPU v7x, 512 devices: a whole 4x8x8 slice. The times are simulated.
512 devices in a mesh: seq: 64 (over y_hi, z, core), tp: 8 (over x, y_lo).
Axes of the slice: x: 4, y: 8 (y_hi: 4, y_lo: 2; y = y_hi * 2 + y_lo), z: 8, core: 2. Of those that a mesh axis runs over, the one named last changes fastest.
Arguments:
- resid: bfloat16 [8192, 2048], P('seq'), may hold values from -1.5 to 1.5
- query: bfloat16 [8192, 1024], P('seq', 'tp'), may hold values from -6 to 6
- key_new: bfloat16 [8192, 1024], P('seq', 'tp'), may hold values from -6 to 6
- value_new: bfloat16 [8192, 1024], P('seq', 'tp'), may hold values from -6 to 6
- key_cache: bfloat16 [1024, 1024], P('seq', 'tp'), may hold values from -6 to 6
- value_cache: bfloat16 [1024, 1024], P('seq', 'tp'), may hold values from -6 to 6
- cache_len: int32 [64], replicated, may hold values from 0 to 16, as said below
- out_weight: bfloat16 [1024, 2048], P('tp'), may hold values from -0.1875 to 0.1875
- norm_gain: bfloat16 [2048], replicated, may hold values from 0.099609375 to 1.8984375
- router: bfloat16 [2048, 64], replicated, may hold values from -2 to 2
- expert_ids: int32 [8192, 6], P('seq'), may hold values from 0 to 63, all different within a row; in each aligned block of 128 rows (0 to 127, 128 to 255, ...) at most 18 rows name the same one
- w_gate: bfloat16 [64, 2048, 1408], P('seq', None, 'tp'), may hold values from -0.125 to 0.125
- w_up: bfloat16 [64, 2048, 1408], P('seq', None, 'tp'), may hold values from -0.125 to 0.125
- w_down: bfloat16 [64, 1408, 2048], P('seq', None, 'tp'), may hold values from -0.15625 to 0.15625
- w_shared_gate: bfloat16 [2048, 1408], P('seq', 'tp'), may hold values from -0.125 to 0.125
- w_shared_up: bfloat16 [2048, 1408], P('seq', 'tp'), may hold values from -0.125 to 0.125
- w_shared_down: bfloat16 [1408, 2048], P('tp', 'seq'), may hold values from -0.15625 to 0.15625
Outputs:
- mixed: bfloat16 [8192, 2048], P('seq', 'tp')
Inputs may be any that keep to these rules, and one draw needn't show every extreme that they name: `cache_len`: some cache block has all 16 rows valid and another has none. `expert_ids`: each row names 6 different experts; the rows of one device name no expert more than 18 times, a bound that some block reaches.
All inputs are finite; a program needn't handle non-finite values.
Results may differ from a plain program's by a relative error of at most 0.013.
Values may be sent and summed in bfloat16 or wider, within the bound.
No kernel may reach another device: no remote copies, remote signals or barrier semaphores. Data moves between devices by JAX's collectives and lax.ppermute only.
A program may use at most 64 MiB of HBM per device.

v0:
```python
import math

import jax
import jax.numpy as jnp
from jax import lax
from jax.sharding import PartitionSpec as P

D = 2048
HD = 128
TOPK = 6


def expert_rows(rows, gate_w, up_w, down_w):
    sources, items = (rows.shape[0], rows.shape[1])
    flat_rows = rows.reshape(sources * items, rows.shape[2])
    gate_pre = jnp.dot(flat_rows, gate_w[0], preferred_element_type=jnp.float32)
    up_pre = jnp.dot(flat_rows, up_w[0], preferred_element_type=jnp.float32)
    inner_units = (
        (jax.nn.silu(gate_pre) * up_pre)
        .astype(jnp.bfloat16)
        .reshape(sources, items, gate_pre.shape[1])
    )
    inner_all = lax.all_gather(inner_units, "tp", axis=2, tiled=True)
    output = jnp.dot(
        inner_all.reshape(sources * items, inner_all.shape[2]),
        down_w[0],
        preferred_element_type=jnp.float32,
    )
    output = output.astype(jnp.bfloat16).reshape(sources, items, down_w.shape[2])
    return lax.all_to_all(output, "seq", split_axis=0, concat_axis=0, tiled=True)


def local(
    resid,
    query,
    key_new,
    value_new,
    key_cache,
    value_cache,
    cache_len,
    out_weight,
    norm_gain,
    router,
    expert_ids,
    w_gate,
    w_up,
    w_down,
    w_shared_gate,
    w_shared_up,
    w_shared_down,
):
    tok_rows = query.shape[0]
    heads_here = query.shape[1] // HD
    block_rows = key_cache.shape[0]
    seq_index = lax.axis_index("seq")
    tp_index = lax.axis_index("tp")
    width = D // lax.axis_size("tp")
    cache_keys, cache_values, fresh_keys, fresh_values = (
        lax.all_gather(key_cache, "seq", axis=0, tiled=True),
        lax.all_gather(value_cache, "seq", axis=0, tiled=True),
        lax.all_gather(key_new, "seq", axis=0, tiled=True),
        lax.all_gather(value_new, "seq", axis=0, tiled=True),
    )
    all_keys = jnp.concatenate([cache_keys, fresh_keys], 0)
    all_values = jnp.concatenate([cache_values, fresh_values], 0)
    span = all_keys.shape[0]
    scores = jnp.einsum(
        "qhd,khd->hqk",
        query.reshape(tok_rows, heads_here, HD),
        all_keys.reshape(span, heads_here, HD),
        preferred_element_type=jnp.float32,
    ) / math.sqrt(HD)
    cache_span = cache_keys.shape[0]
    cache_open = (jnp.arange(block_rows, dtype=jnp.int32)[None, :] < cache_len[:, None]).reshape(
        cache_span
    )
    query_place = seq_index * tok_rows + jnp.arange(tok_rows)
    fresh_open = jnp.arange(fresh_keys.shape[0])[None, :] <= query_place[:, None]
    visible = jnp.concatenate(
        [jnp.broadcast_to(cache_open[None, :], (tok_rows, cache_span)), fresh_open], 1
    )
    scores = jnp.where(visible[None], scores, -jnp.inf)
    top_score = jnp.max(scores, axis=-1, keepdims=True)
    weights = jnp.exp(scores - top_score)
    probs = (weights / jnp.sum(weights, axis=-1, keepdims=True)).astype(jnp.bfloat16)
    attn = jnp.einsum(
        "hqk,khd->qhd",
        probs,
        all_values.reshape(span, heads_here, HD),
        preferred_element_type=jnp.float32,
    )
    attn = attn.astype(jnp.bfloat16).reshape(tok_rows, heads_here * HD)
    partial_out = jnp.dot(attn, out_weight, preferred_element_type=jnp.float32)
    hidden_state = resid.astype(jnp.float32) + lax.psum(partial_out, "tp")
    mean_square = jnp.mean(hidden_state * hidden_state, axis=-1, keepdims=True)
    normed = (hidden_state * lax.rsqrt(mean_square + 1e-06) * norm_gain.astype(jnp.float32)).astype(
        jnp.bfloat16
    )
    own_hidden = lax.dynamic_slice_in_dim(hidden_state, tp_index * width, width, 1)
    logits = jnp.dot(normed, router, preferred_element_type=jnp.float32)
    expert_count = router.shape[1]
    expert_range = jnp.arange(expert_count, dtype=jnp.int32)
    picked = jnp.sum(
        jnp.where(expert_ids[:, :, None] == expert_range[None, None, :], logits[:, None, :], 0.0),
        axis=-1,
    )
    gates = jax.nn.softmax(picked, axis=-1)
    shared_gate = jnp.dot(
        normed,
        lax.all_gather(w_shared_gate, "seq", axis=0, tiled=True),
        preferred_element_type=jnp.float32,
    )
    shared_up = jnp.dot(
        normed,
        lax.all_gather(w_shared_up, "seq", axis=0, tiled=True),
        preferred_element_type=jnp.float32,
    )
    shared_inner = (jax.nn.silu(shared_gate) * shared_up).astype(jnp.bfloat16)
    shared_terms = jnp.dot(
        shared_inner,
        lax.all_gather(w_shared_down, "seq", axis=1, tiled=True),
        preferred_element_type=jnp.float32,
    )
    shared_own = lax.psum_scatter(
        shared_terms.astype(jnp.bfloat16), "tp", scatter_dimension=1, tiled=True
    ).astype(jnp.float32)
    capacity = max(2, 3 * tok_rows * TOPK // (2 * expert_count))
    flat_ids = expert_ids.reshape(tok_rows * TOPK)
    one_hot = (flat_ids[:, None] == expert_range[None, :]).astype(jnp.int32)
    before = jnp.cumsum(one_hot, axis=0) - one_hot
    slot = jnp.sum(one_hot * before, axis=1)
    dest = flat_ids * capacity + slot
    source_row = jnp.repeat(jnp.arange(tok_rows, dtype=jnp.int32), TOPK)
    buffer = jnp.zeros((expert_count * capacity, D), jnp.bfloat16).at[dest].set(normed[source_row])
    buffer = buffer.reshape(expert_count, capacity, D)
    returned = expert_rows(
        lax.all_to_all(buffer, "seq", split_axis=0, concat_axis=0, tiled=True), w_gate, w_up, w_down
    )
    picked_rows = returned.reshape(expert_count * capacity, width)[dest]
    weighted = picked_rows.astype(jnp.float32) * gates.reshape(tok_rows * TOPK)[:, None]
    routed = jnp.sum(weighted.reshape(tok_rows, TOPK, width), axis=1)
    return (own_hidden + shared_own + routed).astype(jnp.bfloat16)


def solution(mesh):
    return jax.shard_map(
        local,
        mesh=mesh,
        in_specs=(
            P("seq", None),
            P("seq", "tp"),
            P("seq", "tp"),
            P("seq", "tp"),
            P("seq", "tp"),
            P("seq", "tp"),
            P(),
            P("tp", None),
            P(),
            P(),
            P("seq", None),
            P("seq", None, "tp"),
            P("seq", None, "tp"),
            P("seq", None, "tp"),
            P("seq", "tp"),
            P("seq", "tp"),
            P("tp", "seq"),
        ),
        out_specs=P("seq", "tp"),
        check_vma=False,
    )
```

profile of v0, /device:TPU:1, one launch (start us, length us, event | category | flops | bytes accessed | tf_op | source)
XLA Modules:
  0.0 866.3 jit_solution(12710250860430260462)
XLA Ops:
  6.5 0.7 all-gather.6.cloned.1.call-update
  7.3 0.7 all-gather.4.cloned.1.call-update
  8.1 0.7 iota_compare_fusion.4
  8.9 91.8 %all_gather.26 = bf16[1024,128]{1,0:T(8,128)(2,1)S(1)} all-gather(bf16[16,128]{1,0:T(8,128)(2,1)} %param.21), channel_id=1, replica_groups=mesh['seq'=64,'tp'=8] {'seq'}, dimensions={0}, use_global_device_ids=true | all-gather | bytes 266240 | tf_op jit(solution)/shard_map/all_gather | solution.py:59
  100.7 77.4 %all_gather.24 = bf16[1024,128]{1,0:T(8,128)(2,1)S(1)} all-gather(bf16[16,128]{1,0:T(8,128)(2,1)} %param.22), channel_id=1, replica_groups=mesh['seq'=64,'tp'=8] {'seq'}, dimensions={0}, use_global_device_ids=true | all-gather | bytes 266240 | tf_op jit(solution)/shard_map/all_gather | solution.py:60
  178.1 0.7 iota_compare_fusion
  178.8 9.6 %fusion.46 = (f32[128]{0:T(128)S(1)}, f32[128,9216]{0,1:T(8,128)S(1)}) fusion(bf16[128,128]{1,0:T(8,128)(2,1)} %param.18, bf16[8192,128]{1,0:T(8,128)(2,1)} %all-gather.6.cloned.1.call-done, bf16[1024,128]{1,0:T(8,128)(2,1)S(1)} %all_gather.26, pred[128,8192]{0,1:T(32,128)(4,1)S(1)} %iota_compare_fusion, pred[9216]{0:T(1024)(128)(4,1)S(1)} %pad.2.clone), kind=kOutput, calls=%fused_computation.71 | convolution fusion | flops 311426944 | bytes 8168960 | tf_op jit(solution)/shard_map/qhd,khd->hqk/dot_general | solution.py:67
  188.5 2.1 copy-done.1
  190.6 1.3 fusion.2
  191.9 5.4 fusion.22
  197.5 0.1 eq.42
  197.6 0.1 eq.38
  197.9 0.1 mul.78
  198.0 0.1 reshape.187
  198.2 2.0 reduce-window.6
  200.2 0.3 slice_reduce_fusion
  200.5 0.1 fusion.30
  200.7 77.4 %all-reduce.2.cloned.1.call-done = f32[128,2048]{1,0:T(8,128)} async-done(((f32[128,2048]{1,0:T(8,128)}), f32[128,2048]{1,0:T(8,128)}) %all-reduce.2.cloned.1.call-update) | async-done | bytes 1048592 | tf_op jit(solution)/shard_map/psum | solution.py:94
  278.0 1.4 multiply_reduce_fusion.1
  279.5 0.2 multiply_convert_fusion
  279.7 23.4 %scatter_custom_fusion = bf16[1152,2048]{1,0:T(8,128)(2,1)} fusion(s32[768]{0:T(1024)S(1)} %fusion.40, bf16[128,2048]{1,0:T(8,128)(2,1)S(1)} %multiply_convert_fusion, s32[1024]{0:T(1024)S(1)} %pad_clamp_fusion.1, bf16[]{:T(256)} %constant.44.clone.1), kind=kCustom, calls=%fused_computation.10 | custom fusion | bytes 4718594 | tf_op jit(solution)/shard_map/scatter | solution.py:134
  303.1 7.6 reshape.188
  310.7 168.5 %all_to_all.10 = bf16[64,18,2048]{2,1,0:T(8,128)(2,1)} all-to-all(bf16[64,18,2048]{2,1,0:T(8,128)(2,1)} %reshape.188), channel_id=1, replica_groups=mesh['seq'=64,'tp'=8] {'seq'}, dimensions={0} | all-to-all | bytes 9437184 | tf_op jit(solution)/shard_map/all_to_all | solution.py:137
  479.1 7.8 reshape.189
  486.9 4.2 fusion.26
  491.2 1.7 fusion.5
  492.9 1.1 copy.40
  494.0 1.4 reshape.190
  495.4 2.8 copy.41
  498.3 97.7 %all_gather.28 = bf16[2048,176]{1,0:T(8,128)(2,1)S(1)} all-gather(bf16[32,176]{1,0:T(8,128)(2,1)S(1)} %copy-done.5), channel_id=1, replica_groups=mesh['seq'=64,'tp'=8] {'seq'}, dimensions={0}, use_global_device_ids=true | all-gather | bytes 732160 | tf_op jit(solution)/shard_map/all_gather | solution.py:110
  596.0 84.4 %all_gather.29 = bf16[2048,176]{1,0:T(8,128)(2,1)S(1)} all-gather(bf16[32,176]{1,0:T(8,128)(2,1)S(1)} %copy-done.6), channel_id=1, replica_groups=mesh['seq'=64,'tp'=8] {'seq'}, dimensions={0}, use_global_device_ids=true | all-gather | bytes 732160 | tf_op jit(solution)/shard_map/all_gather | solution.py:115
  680.4 87.9 %all_gather.30 = bf16[176,2048]{0,1:T(8,128)(2,1)} all-gather(bf16[176,32]{0,1:T(8,128)(2,1)S(1)} %copy-done.7), channel_id=1, replica_groups=mesh['seq'=64,'tp'=8] {'seq'}, dimensions={1}, use_global_device_ids=true | all-gather | bytes 732160 | tf_op jit(solution)/shard_map/all_gather | solution.py:121
  768.3 0.5 fusion.47
  768.9 13.3 %copy.42 = bf16[64,18,1408]{2,1,0:T(8,128)(2,1)} copy(bf16[64,18,1408]{0,1,2:T(8,128)(2,1)} %all-gather.8.cloned.1.call-done) | data formatting | bytes 6488064 | tf_op jit(solution)/shard_map/all_gather | solution.py:23
  782.2 5.8 reshape.191
  788.0 3.8 convolution_convert_fusion
  791.8 2.1 reshape.192
  793.8 11.8 %all-to-all-start.1 = ((bf16[64,18,256]{2,1,0:T(8,128)(2,1)}), bf16[64,18,256]{2,1,0:T(8,128)(2,1)}, u32[]{:S(2)}, u32[]{:S(2)}) async-start(bf16[64,18,256]{2,1,0:T(8,128)(2,1)} %reshape.192), calls=%async_computation.2 | async-start | bytes 1572864 | tf_op jit(solution)/shard_map/all_to_all | solution.py:30
  805.7 3.2 convolution_convert_fusion.1
  809.0 1.3 fusion.48
  810.3 0.1 copy.43
  810.5 20.2 %all-to-all-done.1 = bf16[64,18,256]{2,1,0:T(8,128)(2,1)} async-done(((bf16[64,18,256]{2,1,0:T(8,128)(2,1)}), bf16[64,18,256]{2,1,0:T(8,128)(2,1)}, u32[]{:S(2)}, u32[]{:S(2)}) %all-to-all-start.1) | async-done | bytes 589856 | tf_op jit(solution)/shard_map/all_to_all | solution.py:30
  830.7 1.3 reshape.193
  832.0 3.3 gather_fusion
  835.3 1.1 reshape.194
  836.4 0.4 multiply_reduce_fusion
  836.8 21.5 %reduce-scatter.2.cloned.1.call-done = bf16[128,256]{1,0:T(8,128)(2,1)} async-done(((bf16[128,2048]{1,0:T(8,128)(2,1)}), bf16[128,256]{1,0:T(8,128)(2,1)}) %reduce-scatter.2.cloned.1.call-update) | async-done | bytes 65552 | tf_op jit(solution)/shard_map/reduce_scatter | solution.py:124
  858.3 1.5 add_convert_fusion
  (53 shorter events, 0.9 us)
Async XLA Ops:
  6.5 781.4 %copy-start = (bf16[1,1408,256]{2,1,0:T(8,128)(2,1)S(1)}, bf16[1,1408,256]{2,1,0:T(8,128)(2,1)}, u32[]{:S(2)}) copy-start(bf16[1,1408,256]{2,1,0:T(8,128)(2,1)} %param.30) | copy-start | bytes 2162692
  6.5 172.3 %all-gather.6.cloned.1.call-start = ((), (), s32[]{:S(2)}) async-start(), calls=%async_computation.4 | async-start | bytes 2129920 | tf_op jit(solution)/shard_map/all_gather | solution.py:61
  7.3 184.6 %all-gather.4.cloned.1.call-start = ((), (), s32[]{:S(2)}) async-start(), calls=%async_computation.3 | async-start | bytes 2129920 | tf_op jit(solution)/shard_map/all_gather | solution.py:62
  8.0 270.0 %all-reduce.2.cloned.1.call-start = ((), (), s32[]{:S(2)}) async-start(), calls=%async_computation.5 | async-start | bytes 2097152 | tf_op jit(solution)/shard_map/psum | solution.py:94
  188.5 2.1 copy-start.1
  188.5 3.4 copy-start.11
  191.8 5.5 copy-start.4
  191.8 5.9 copy-start.8
  191.9 86.2 %copy-start.3 = (bf16[128,2048]{1,0:T(8,128)(2,1)S(1)}, bf16[128,2048]{1,0:T(8,128)(2,1)}, u32[]{:S(2)}) copy-start(bf16[128,2048]{1,0:T(8,128)(2,1)} %param.17) | copy-start | bytes 1572868
  197.3 571.6 %all-gather.8.cloned.1.call-start = ((), (), s32[]{:S(2)}) async-start(), calls=%async_computation.7 | async-start | bytes 9732096 | tf_op jit(solution)/shard_map/all_gather | solution.py:23
  479.1 7.8 copy-start.9
  486.9 4.2 copy-start.2
  486.9 4.2 copy-start.10
  492.9 5.4 copy-start.5
  492.9 103.1 %copy-start.6 = (bf16[32,176]{1,0:T(8,128)(2,1)S(1)}, bf16[32,176]{1,0:T(8,128)(2,1)}, u32[]{:S(2)}) copy-start(bf16[32,176]{1,0:T(8,128)(2,1)} %param.32) | copy-start | bytes 33796
  492.9 187.5 %copy-start.7 = (bf16[176,32]{0,1:T(8,128)(2,1)S(1)}, bf16[176,32]{0,1:T(8,128)(2,1)}, u32[]{:S(2)}) copy-start(bf16[176,32]{0,1:T(8,128)(2,1)} %param.33) | copy-start | bytes 33796
  793.8 36.9 %all-to-all-start.1 = ((bf16[64,18,256]{2,1,0:T(8,128)(2,1)}), bf16[64,18,256]{2,1,0:T(8,128)(2,1)}, u32[]{:S(2)}, u32[]{:S(2)}) async-start(bf16[64,18,256]{2,1,0:T(8,128)(2,1)} %reshape.192), calls=%async_computation.2 | async-start | bytes 1572864 | tf_op jit(solution)/shard_map/all_to_all | solution.py:30
  805.7 52.6 %reduce-scatter.2.cloned.1.call-start = ((), (), s32[]{:S(2)}) async-start(), calls=%async_computation.6 | async-start | bytes 589824 | tf_op jit(solution)/shard_map/reduce_scatter | solution.py:124
Sparse Core Ops, SparseCore 0:
  10.7 90.6 all-gather.5
  104.7 80.3 all-gather.3
  197.4 80.5 all-reduce.1
  498.4 230.1 all-gather.7
  809.1 49.1 reduce-scatter.1
where the time goes:
time: 872 us; the launch traced here: 866 us
  blocking collectives  608 us (70%)
  waiting for transfers between devices  121 us (14%)
  local copies, waits for them, and re-layouts  74.3 us (9%)
  matrix products  29.7 us (3%)
  between operations  13.5 us (2%)
  starting transfers between devices  12 us (1%)
    all_to_all x1, blocking collectives, local(): lax.all_to_all(buffer, 'seq', split_axis=0, concat_axis=0, tiled=True)  168 us
    all_gather x1, blocking collectives, local(): lax.all_gather(w_shared_gate, 'seq', axis=0, tiled=True)  97.7 us
    all_gather x1, blocking collectives, local(): lax.all_gather(key_cache, 'seq', axis=0, tiled=True)  91.8 us
    all_gather x1, blocking collectives, local(): lax.all_gather(w_shared_down, 'seq', axis=1, tiled=True)  87.9 us
    all_gather x1, blocking collectives, local(): lax.all_gather(w_shared_up, 'seq', axis=0, tiled=True)  84.4 us
    all_gather x1, blocking collectives, local(): lax.all_gather(value_cache, 'seq', axis=0, tiled=True)  77.4 us
    psum x1, waiting for transfers between devices, local(): hidden_state = resid.astype(jnp.float32) + lax.psum(partial_out, 'tp')  77.4 us
    scatter x1, local copies, waits for them, and re-layouts, local(): jnp.zeros((expert_count * capacity, D), jnp.bfloat16).at[dest]  23.4 us
  transfers between devices with their start and end apart: 6, of which 3 were waited for; matrix products, arithmetic and copies ran while one was open for 3% of the time, Pallas kernels for 0%

commit v1 on v0

v1 whole, which is shorter than its diff:
```python
import math

import jax
import jax.numpy as jnp
import numpy as np
from jax import lax
from jax.sharding import Mesh
from jax.sharding import PartitionSpec as P

D = 2048
HD = 128
TOPK = 6
CAP = 18

SEQ = ("yh", "z", "c")
TP = ("x", "yl")


def gather_seq(x):
    g = lax.all_gather(x, "yh", axis=0)
    g = lax.all_gather(g, "z", axis=0)
    g = lax.all_gather(g, "c", axis=0)
    return g


def local(
    resid,
    query,
    key_new,
    value_new,
    key_cache,
    value_cache,
    cache_len,
    out_weight,
    norm_gain,
    router,
    expert_ids,
    w_gate,
    w_up,
    w_down,
    w_shared_gate,
    w_shared_up,
    w_shared_down,
):
    tok_rows = query.shape[0]
    block_rows = key_cache.shape[0]
    n_yh, n_z, n_c = (lax.axis_size(a) for a in SEQ)
    n_x, n_yl = (lax.axis_size(a) for a in TP)
    n_seq = n_yh * n_z * n_c
    n_tp = n_x * n_yl
    seq_index = (lax.axis_index("yh") * n_z + lax.axis_index("z")) * n_c + lax.axis_index("c")
    tp_index = lax.axis_index("x") * n_yl + lax.axis_index("yl")
    width = D // n_tp

    ow_all = lax.all_gather(out_weight, TP, axis=0)
    wpack = jnp.stack([w_shared_gate, w_shared_up, w_shared_down.T], 0)
    wg = gather_seq(wpack)
    wg = jnp.transpose(wg, (2, 1, 0, 3, 4, 5)).reshape(n_seq, 3, wpack.shape[1], wpack.shape[2])
    sg_w = wg[:, 0].reshape(n_seq * wpack.shape[1], wpack.shape[2])
    su_w = wg[:, 1].reshape(n_seq * wpack.shape[1], wpack.shape[2])
    sd_t = wg[:, 2].reshape(n_tp, n_seq // n_tp, wpack.shape[1], wpack.shape[2])
    sd_own = lax.all_to_all(sd_t, TP, split_axis=0, concat_axis=0, tiled=True)

    kv = jnp.concatenate([key_cache, key_new, value_cache, value_new], 0)
    kvg = gather_seq(kv).reshape(n_seq, kv.shape[0], HD)
    pos = jnp.arange(n_seq, dtype=jnp.int32)
    src = (pos % n_yh) * (n_z * n_c) + ((pos // n_yh) % n_z) * n_c + pos // (n_yh * n_z)
    ck = kvg[:, :block_rows].reshape(n_seq * block_rows, HD)
    nk = kvg[:, block_rows:block_rows + tok_rows].reshape(n_seq * tok_rows, HD)
    cv = kvg[:, block_rows + tok_rows:2 * block_rows + tok_rows].reshape(n_seq * block_rows, HD)
    nv = kvg[:, 2 * block_rows + tok_rows:].reshape(n_seq * tok_rows, HD)

    scale = 1.0 / math.sqrt(HD)
    s_c = jnp.dot(query, ck.T, preferred_element_type=jnp.float32) * scale
    s_n = jnp.dot(query, nk.T, preferred_element_type=jnp.float32) * scale
    c_open = (
        jnp.arange(block_rows, dtype=jnp.int32)[None, :] < cache_len[src][:, None]
    ).reshape(n_seq * block_rows)
    key_place = (src[:, None] * tok_rows + jnp.arange(tok_rows, dtype=jnp.int32)[None, :]).reshape(
        n_seq * tok_rows
    )
    query_place = seq_index * tok_rows + jnp.arange(tok_rows, dtype=jnp.int32)
    n_open = key_place[None, :] <= query_place[:, None]
    s_c = jnp.where(c_open[None, :], s_c, -jnp.inf)
    s_n = jnp.where(n_open, s_n, -jnp.inf)
    top = jnp.maximum(jnp.max(s_c, axis=-1, keepdims=True), jnp.max(s_n, axis=-1, keepdims=True))
    e_c = jnp.exp(s_c - top)
    e_n = jnp.exp(s_n - top)
    total = jnp.sum(e_c, axis=-1, keepdims=True) + jnp.sum(e_n, axis=-1, keepdims=True)
    p_c = (e_c / total).astype(jnp.bfloat16)
    p_n = (e_n / total).astype(jnp.bfloat16)
    attn = jnp.dot(p_c, cv, preferred_element_type=jnp.float32) + jnp.dot(
        p_n, nv, preferred_element_type=jnp.float32
    )
    attn = attn.astype(jnp.bfloat16)

    attn_all = lax.all_gather(attn, TP, axis=0)
    hidden_state = resid.astype(jnp.float32) + jnp.einsum(
        "tqd,tdn->qn", attn_all, ow_all, preferred_element_type=jnp.float32
    )
    mean_square = jnp.mean(hidden_state * hidden_state, axis=-1, keepdims=True)
    normed = (hidden_state * lax.rsqrt(mean_square + 1e-06) * norm_gain.astype(jnp.float32)).astype(
        jnp.bfloat16
    )
    own_hidden = lax.dynamic_slice_in_dim(hidden_state, tp_index * width, width, 1)
    own_normed = lax.dynamic_slice_in_dim(normed, tp_index * width, width, 1)

    logits = jnp.dot(normed, router, preferred_element_type=jnp.float32)
    expert_count = router.shape[1]
    expert_range = jnp.arange(expert_count, dtype=jnp.int32)
    picked = jnp.sum(
        jnp.where(expert_ids[:, :, None] == expert_range[None, None, :], logits[:, None, :], 0.0),
        axis=-1,
    )
    gates = jax.nn.softmax(picked, axis=-1)

    shared_gate = jnp.dot(normed, sg_w, preferred_element_type=jnp.float32)
    shared_up = jnp.dot(normed, su_w, preferred_element_type=jnp.float32)
    shared_inner = (jax.nn.silu(shared_gate) * shared_up).astype(jnp.bfloat16)
    inner_all = lax.all_gather(shared_inner, TP, axis=0)
    shared_own = jnp.einsum(
        "tqf,tsjf->qsj", inner_all, sd_own, preferred_element_type=jnp.float32
    ).reshape(tok_rows, width)

    flat_ids = expert_ids.reshape(tok_rows * TOPK)
    one_hot = (flat_ids[:, None] == expert_range[None, :]).astype(jnp.int32)
    before = jnp.cumsum(one_hot, axis=0) - one_hot
    slot = jnp.sum(one_hot * before, axis=1)
    dest = flat_ids * CAP + slot
    slots = expert_count * CAP
    place = (dest[None, :] == jnp.arange(slots, dtype=jnp.int32)[:, None]).reshape(
        slots, tok_rows, TOPK
    )
    dispatch = jnp.any(place, axis=-1).astype(jnp.bfloat16)
    buffer = jnp.dot(dispatch, own_normed, preferred_element_type=jnp.float32).astype(jnp.bfloat16)
    buffer = buffer.reshape(expert_count, CAP, width)
    recv = lax.all_to_all(buffer, SEQ, split_axis=0, concat_axis=0, tiled=True)
    rows_all = lax.all_gather(recv, TP, axis=0)
    ff = w_gate.shape[2]
    gate_pre = jnp.einsum(
        "tsrc,tcf->srf", rows_all, w_gate[0].reshape(n_tp, width, ff), preferred_element_type=jnp.float32
    )
    up_pre = jnp.einsum(
        "tsrc,tcf->srf", rows_all, w_up[0].reshape(n_tp, width, ff), preferred_element_type=jnp.float32
    )
    inner = (jax.nn.silu(gate_pre) * up_pre).astype(jnp.bfloat16)
    inner_r = lax.all_gather(inner, TP, axis=0)
    out = jnp.einsum(
        "tsrf,tfn->srn",
        inner_r,
        w_down[0].reshape(n_tp, ff, w_down.shape[2]),
        preferred_element_type=jnp.float32,
    ).astype(jnp.bfloat16)
    returned = lax.all_to_all(out, SEQ, split_axis=0, concat_axis=0, tiled=True)
    picked_rows = returned.reshape(slots, width)[dest]
    weighted = picked_rows.astype(jnp.float32) * gates.reshape(tok_rows * TOPK)[:, None]
    routed = jnp.sum(weighted.reshape(tok_rows, TOPK, width), axis=1)
    return (own_hidden + shared_own + routed).astype(jnp.bfloat16)


def solution(mesh):
    n_seq, n_tp = mesh.devices.shape
    fine = Mesh(mesh.devices.reshape(n_seq // 16, 8, 2, n_tp // 2, 2), SEQ + TP)
    return jax.shard_map(
        local,
        mesh=fine,
        in_specs=(
            P(SEQ, None),
            P(SEQ, TP),
            P(SEQ, TP),
            P(SEQ, TP),
            P(SEQ, TP),
            P(SEQ, TP),
            P(),
            P(TP, None),
            P(),
            P(),
            P(SEQ, None),
            P(SEQ, None, TP),
            P(SEQ, None, TP),
            P(SEQ, None, TP),
            P(SEQ, TP),
            P(SEQ, TP),
            P(TP, SEQ),
        ),
        out_specs=P(SEQ, TP),
        check_vma=False,
    )
```

time: 872 us -> 580 us (0.67)
  blocking collectives: 608 us -> 129 us
  waiting for transfers between devices: 121 us -> 360 us
  local copies, waits for them, and re-layouts: 74.3 us -> 23.8 us
    all_gather x5 -> x4, blocking collectives: 439 us -> 90.6 us  [the longest x1 35.2 us: local(): inner_all = lax.all_gather(shared_inner, TP, axis=0)]
    all_gather x3 -> x7, waiting for transfers between devices: 0.06 us -> 340 us  [the longest x1 112 us: local(): rows_all = lax.all_gather(recv, TP, axis=0)]
    all_to_all x1, blocking collectives: 168 us -> 38.4 us  [local(): recv = lax.all_to_all(buffer, SEQ, split_axis=0, concat_axis=0, tiled=True)]
    psum x1 -> x0, waiting for transfers between devices: 77.4 us -> none  [local(): hidden_state = resid.astype(jnp.float32) + lax.psum(partial_out, 'tp')]
    reshape x8 -> x3, local copies, waits for them, and re-layouts: 28.9 us -> 1.52 us  [the longest x1 1.25 us: local(): buffer = buffer.reshape(expert_count, CAP, width)]
    scatter x1 -> x0, local copies, waits for them, and re-layouts: 23.4 us -> none  [local(): jnp.zeros((expert_count * capacity, D), jnp.bfloat16).at[dest]]
    reduce_scatter x1 -> x0, waiting for transfers between devices: 21.5 us -> none  [local(): lax.psum_scatter(shared_terms.astype(jnp.bfloat16), 'tp', scatter_dimensi...]
    all_gather x1 -> x0, local copies, waits for them, and re-layouts: 13.3 us -> none  [expert_rows(): inner_all = lax.all_gather(inner_units, 'tp', axis=2, tiled=True)]
  transfers between devices with their start and end apart: 6 -> 9, of which waited for: 3 -> 8; matrix products, arithmetic and copies ran while one was open for 3% -> 8% of each run, Pallas kernels for 0% -> 0%
where the time goes in v1:
time: 580 us; the launch traced here: 575 us
  waiting for transfers between devices  360 us (62%)
  blocking collectives  129 us (22%)
  local copies, waits for them, and re-layouts  23.8 us (4%)
  matrix products  23.4 us (4%)
  starting transfers between devices  17.1 us (3%)
  between operations  13.8 us (2%)
  other arithmetic  7.02 us (1%)
    all_gather x1, waiting for transfers between devices, local(): rows_all = lax.all_gather(recv, TP, axis=0)  112 us
    all_gather x1, waiting for transfers between devices, local(): inner_r = lax.all_gather(inner, TP, axis=0)  78 us
    all_gather x1, waiting for transfers between devices, local(): ow_all = lax.all_gather(out_weight, TP, axis=0)  67.6 us
    all_gather x2, waiting for transfers between devices, gather_seq(): g = lax.all_gather(g, 'z', axis=0)  57.3 us
    all_to_all x1, blocking collectives, local(): recv = lax.all_to_all(buffer, SEQ, split_axis=0, concat_axis=0, tiled=True)  38.4 us
    all_gather x1, blocking collectives, local(): inner_all = lax.all_gather(shared_inner, TP, axis=0)  35.2 us
    all_gather x2, blocking collectives, gather_seq(): g = lax.all_gather(x, 'yh', axis=0)  30.3 us
    all_gather x2, waiting for transfers between devices, gather_seq(): g = lax.all_gather(g, 'c', axis=0)  25.7 us
  transfers between devices with their start and end apart: 9, of which 8 were waited for; matrix products, arithmetic and copies ran while one was open for 8% of the time, Pallas kernels for 0%

profile of v1, /device:TPU:1, one launch (start us, length us, event | category | flops | bytes accessed | tf_op | source)
XLA Modules:
  0.0 574.5 jit_solution(5562629001401897351)
XLA Ops:
  6.6 0.9 pad_maximum_fusion
  7.4 16.1 %all-gather = bf16[1152,128]{1,0:T(8,128)(2,1)} all-gather(bf16[288,128]{1,0:T(8,128)(2,1)S(1)} %pad_maximum_fusion), channel_id=2, replica_groups=mesh['yh'=4,'z'=8,'c'=2,'x'=4,'yl'=2] {'yh'}, dimensions={0}, use_global_device_ids=true | all-gather | bytes 368640 | tf_op jit(solution)/shard_map/all_gather | solution.py:20
  23.6 46.0 %all-gather.19.cloned.1.call-done = bf16[32,288,128]{2,1,0:T(8,128)(2,1)} async-done(((bf16[4,288,128]{2,1,0:T(8,128)(2,1)}), bf16[32,288,128]{2,1,0:T(8,128)(2,1)}) %all-gather.19.cloned.1.call-update) | async-done | bytes 2359312 | tf_op jit(solution)/shard_map/all_gather | solution.py:21
  69.7 0.7 all-gather.23.cloned.1.call-update
  70.4 0.8 pad_maximum_fusion.1
  71.2 14.2 %all-gather.5 = bf16[12,32,176]{2,1,0:T(8,128)(2,1)} all-gather(bf16[3,32,176]{2,1,0:T(8,128)(2,1)S(1)} %pad_maximum_fusion.1), channel_id=7, replica_groups=mesh['yh'=4,'z'=8,'c'=2,'x'=4,'yl'=2] {'yh'}, dimensions={0}, use_global_device_ids=true | all-gather | bytes 168960 | tf_op jit(solution)/shard_map/all_gather | solution.py:20
  86.1 0.8 gather_fusion
  87.1 1.8 reduce-window.6
  89.5 0.6 fusion.3
  90.1 7.9 %all-gather.21.cloned.1.call-done = bf16[16,4,288,128]{3,2,1,0:T(8,128)(2,1)} async-done(((bf16[8,4,288,128]{3,2,1,0:T(8,128)(2,1)}), bf16[16,4,288,128]{3,2,1,0:T(8,128)(2,1)}) %all-gather.21.cloned.1.call-update) | async-done | bytes 4718608 | tf_op jit(solution)/shard_map/all_gather | solution.py:22
  98.1 2.7 fusion.40
  100.8 1.1 fusion.39
  101.9 0.3 fusion.42
  102.2 1.3 fusion.43
  103.5 1.1 fusion.2
  104.8 1.0 fusion.5
  105.8 0.3 fusion.11
  106.1 25.1 %all-gather.3 = bf16[1024,128]{1,0:T(8,128)(2,1)S(1)} all-gather(bf16[128,128]{1,0:T(8,128)(2,1)S(1)} %fusion.11), channel_id=5, replica_groups=mesh['yh'=4,'z'=8,'c'=2,'x'=4,'yl'=2] {'x','yl'}, dimensions={0}, use_global_device_ids=true | all-gather | bytes 294912 | tf_op jit(solution)/shard_map/all_gather | solution.py:97
  131.2 67.6 %all-gather.23.cloned.1.call-done = bf16[1024,2048]{1,0:T(8,128)(2,1)} async-done(((bf16[128,2048]{1,0:T(8,128)(2,1)}), bf16[1024,2048]{1,0:T(8,128)(2,1)}) %all-gather.23.cloned.1.call-update) | async-done | bytes 4194320 | tf_op jit(solution)/shard_map/all_gather | solution.py:55
  198.8 3.0 multiply_reduce_fusion.1
  202.0 1.1 convolution_convert_fusion
  203.1 1.2 reshape.312
  204.4 38.4 %all_to_all.15 = bf16[64,18,256]{2,1,0:T(8,128)(2,1)S(1)} all-to-all(bf16[64,18,256]{2,1,0:T(8,128)(2,1)S(1)} %reshape.312), channel_id=1, replica_groups=mesh['yh'=4,'z'=8,'c'=2,'x'=4,'yl'=2] {'yh','z','c'}, dimensions={0} | all-to-all | bytes 1179648 | tf_op jit(solution)/shard_map/all_to_all | solution.py:137
  242.8 0.9 copy.73
  243.8 11.2 %all-gather.25.cloned.1.call-done = bf16[32,3,32,176]{3,2,1,0:T(8,128)(2,1)} async-done(((bf16[4,3,32,176]{3,2,1,0:T(8,128)(2,1)}), bf16[32,3,32,176]{3,2,1,0:T(8,128)(2,1)}) %all-gather.25.cloned.1.call-update) | async-done | bytes 1081360 | tf_op jit(solution)/shard_map/all_gather | solution.py:21
  255.3 2.2 copy.84
  257.5 1.1 copy.85
  258.6 112.0 %all-gather.29.cloned.1.call-done = bf16[512,18,256]{2,0,1:T(8,128)(2,1)} async-done(((bf16[64,18,256]{2,0,1:T(8,128)(2,1)}), bf16[512,18,256]{2,0,1:T(8,128)(2,1)}) %all-gather.29.cloned.1.call-update) | async-done | bytes 4718608 | tf_op jit(solution)/shard_map/all_gather | solution.py:138
  370.5 4.1 convolution_bitcast_fusion.3
  374.7 2.3 fusion.7
  377.1 17.7 %all-gather.27.cloned.1.call-done = bf16[16,4,3,32,176]{4,3,2,1,0:T(8,128)(2,1)} async-done(((bf16[8,4,3,32,176]{4,3,2,1,0:T(8,128)(2,1)}), bf16[16,4,3,32,176]{4,3,2,1,0:T(8,128)(2,1)}) %all-gather.27.cloned.1.call-update) | async-done | bytes 2162704 | tf_op jit(solution)/shard_map/all_gather | solution.py:22
  394.8 2.3 copy.65
  397.1 1.8 fusion.41
  398.9 4.2 all-to-all-start
  403.4 19.1 %all-to-all-done = bf16[8,8,32,176]{3,2,1,0:T(8,128)(2,1)} async-done(((bf16[8,8,32,176]{3,2,1,0:T(8,128)(2,1)}), bf16[8,8,32,176]{3,2,1,0:T(8,128)(2,1)}, u32[]{:S(2)}, u32[]{:S(2)}) %all-to-all-start) | async-done | bytes 720928 | tf_op jit(solution)/shard_map/all_to_all | solution.py:62
  422.5 4.0 copy.66
  426.5 0.5 fusion.44
  427.0 1.7 fusion.10
  428.7 78.0 %all-gather.31.cloned.1.call-done = bf16[512,18,176]{2,0,1:T(8,128)(2,1)} async-done(((bf16[64,18,176]{2,0,1:T(8,128)(2,1)}), bf16[512,18,176]{2,0,1:T(8,128)(2,1)}) %all-gather.31.cloned.1.call-update) | async-done | bytes 3244048 | tf_op jit(solution)/shard_map/all_gather | solution.py:147
  506.8 3.7 fusion.8
  510.4 1.2 copy.76
  511.6 12.4 %all-to-all-start.2 = ((bf16[64,18,256]{2,1,0:T(8,128)(2,1)}), bf16[64,18,256]{2,1,0:T(8,128)(2,1)S(1)}, u32[]{:S(2)}, u32[]{:S(2)}) async-start(bf16[64,18,256]{2,1,0:T(8,128)(2,1)} %copy.76), calls=%async_computation.2 | async-start | bytes 1572864 | tf_op jit(solution)/shard_map/all_to_all | solution.py:154
  524.1 35.2 %all-gather.8 = bf16[1024,176]{0,1:T(8,128)(2,1)S(1)} all-gather(bf16[128,176]{0,1:T(8,128)(2,1)S(1)} %fusion.10), channel_id=10, replica_groups=mesh['yh'=4,'z'=8,'c'=2,'x'=4,'yl'=2] {'x','yl'}, dimensions={0}, use_global_device_ids=true | all-gather | bytes 405504 | tf_op jit(solution)/shard_map/all_gather | solution.py:120
  559.3 2.7 fusion.45
  562.2 1.3 fusion.46
  563.9 2.7 gather_fusion.1
  566.6 0.4 multiply_reduce_fusion
  567.0 0.7 add_convert_fusion
  (67 shorter events, 3.1 us)
Async XLA Ops:
  6.5 500.2 %copy-start = (bf16[1,1408,256]{2,1,0:T(8,128)(2,1)S(1)}, bf16[1,1408,256]{2,1,0:T(8,128)(2,1)}, u32[]{:S(2)}) copy-start(bf16[1,1408,256]{2,1,0:T(8,128)(2,1)} %param.30) | copy-start | bytes 2162692
  6.5 79.0 %copy-start.6 = (s32[128,6]{0,1:T(8,128)S(1)}, s32[128,6]{0,1:T(8,128)}, u32[]{:S(2)}) copy-start(s32[128,6]{0,1:T(8,128)} %param.27) | copy-start | bytes 9220
  6.5 79.5 %copy-start.1 = (s32[64]{0:T(128)S(1)}, s32[64]{0:T(128)}, u32[]{:S(2)}) copy-start(s32[64]{0:T(128)} %param.23) | copy-start | bytes 772
  6.5 80.5 %copy-start.7 = (bf16[2048]{0:T(1024)(128)(2,1)S(1)}, bf16[2048]{0:T(1024)(128)(2,1)}, u32[]{:S(2)}) copy-start(bf16[2048]{0:T(1024)(128)(2,1)} %param.25) | copy-start | bytes 12292
  6.5 63.1 %all-gather.19.cloned.1.call-start = ((), (), s32[]{:S(2)}) async-start(), calls=%async_computation.3 | async-start | bytes 2654208 | tf_op jit(solution)/shard_map/all_gather | solution.py:21
  23.6 74.5 %all-gather.21.cloned.1.call-start = ((), (), s32[]{:S(2)}) async-start(), calls=%async_computation.4 | async-start | bytes 7077888 | tf_op jit(solution)/shard_map/all_gather | solution.py:22
  69.6 129.2 %all-gather.23.cloned.1.call-start = ((), (), s32[]{:S(2)}) async-start(), calls=%async_computation.5 | async-start | bytes 4718592 | tf_op jit(solution)/shard_map/all_gather | solution.py:55
  70.4 184.6 %all-gather.25.cloned.1.call-start = ((), (), s32[]{:S(2)}) async-start(), calls=%async_computation.6 | async-start | bytes 1769472 | tf_op jit(solution)/shard_map/all_gather | solution.py:21
  85.5 285.1 %all-gather.29.cloned.1.call-start = ((), (), s32[]{:S(2)}) async-start(), calls=%async_computation.8 | async-start | bytes 5308416 | tf_op jit(solution)/shard_map/all_gather | solution.py:138
  98.1 3.8 copy-start.5
  104.8 94.0 %copy-start.4 = (bf16[128,2048]{1,0:T(8,128)(2,1)S(1)}, bf16[128,2048]{1,0:T(8,128)(2,1)}, u32[]{:S(2)}) copy-start(bf16[128,2048]{1,0:T(8,128)(2,1)} %param.17) | copy-start | bytes 1572868
  242.8 14.7 %copy-start.2 = (bf16[1,2048,176]{1,2,0:T(8,128)(2,1)S(1)}, bf16[1,2048,176]{1,2,0:T(8,128)(2,1)}, u32[]{:S(2)}) copy-start(bf16[1,2048,176]{1,2,0:T(8,128)(2,1)} %param.29) | copy-start | bytes 2162692
  243.7 151.1 %all-gather.27.cloned.1.call-start = ((), (), s32[]{:S(2)}) async-start(), calls=%async_computation.7 | async-start | bytes 4718592 | tf_op jit(solution)/shard_map/all_gather | solution.py:22
  255.0 251.7 %all-gather.31.cloned.1.call-start = ((), (), s32[]{:S(2)}) async-start(), calls=%async_computation.9 | async-start | bytes 5308416 | tf_op jit(solution)/shard_map/all_gather | solution.py:147
  370.5 4.1 copy-start.3
  370.5 4.2 copy-start.8
  398.9 23.5 %all-to-all-start = ((bf16[8,8,32,176]{3,2,1,0:T(8,128)(2,1)}), bf16[8,8,32,176]{3,2,1,0:T(8,128)(2,1)}, u32[]{:S(2)}, u32[]{:S(2)}) async-start(bf16[8,8,32,176]{3,2,1,0:T(8,128)(2,1)} %bitcast.127), calls=%async_computation | async-start | bytes 2097152 | tf_op jit(solution)/shard_map/all_to_all | solution.py:62
  511.6 52.0 %all-to-all-start.2 = ((bf16[64,18,256]{2,1,0:T(8,128)(2,1)}), bf16[64,18,256]{2,1,0:T(8,128)(2,1)S(1)}, u32[]{:S(2)}, u32[]{:S(2)}) async-start(bf16[64,18,256]{2,1,0:T(8,128)(2,1)} %copy.76), calls=%async_computation.2 | async-start | bytes 1572864 | tf_op jit(solution)/shard_map/all_to_all | solution.py:154
Sparse Core Ops, SparseCore 0:
  23.7 45.9 all-gather.18
  71.7 26.3 all-gather.20
  100.1 98.6 all-gather.22
  200.7 54.2 all-gather.24
  256.9 113.5 all-gather.28
  372.5 22.2 all-gather.26
  396.9 109.8 all-gather.30

commit v2 on v1

--- a/solution.py
+++ b/solution.py
@@ -21,6 +21,13 @@
     g = lax.all_gather(g, "z", axis=0)
     g = lax.all_gather(g, "c", axis=0)
     return g
+
+
+def tp_blocks(x, n_tp):
+    out = [x]
+    for k in range(1, n_tp):
+        out.append(lax.ppermute(x, TP, [(j, (j + k) % n_tp) for j in range(n_tp)]))
+    return out
 
 
 def local(
@@ -52,7 +59,7 @@
     tp_index = lax.axis_index("x") * n_yl + lax.axis_index("yl")
     width = D // n_tp
 
-    ow_all = lax.all_gather(out_weight, TP, axis=0)
+    ow_blocks = tp_blocks(out_weight, n_tp)
     wpack = jnp.stack([w_shared_gate, w_shared_up, w_shared_down.T], 0)
     wg = gather_seq(wpack)
     wg = jnp.transpose(wg, (2, 1, 0, 3, 4, 5)).reshape(n_seq, 3, wpack.shape[1], wpack.shape[2])
@@ -94,10 +101,11 @@
     )
     attn = attn.astype(jnp.bfloat16)
 
-    attn_all = lax.all_gather(attn, TP, axis=0)
-    hidden_state = resid.astype(jnp.float32) + jnp.einsum(
-        "tqd,tdn->qn", attn_all, ow_all, preferred_element_type=jnp.float32
-    )
+    attn_blocks = tp_blocks(attn, n_tp)
+    projected = sum(
+        jnp.dot(a, w, preferred_element_type=jnp.float32) for a, w in zip(attn_blocks, ow_blocks)
+    )
+    hidden_state = resid.astype(jnp.float32) + projected
     mean_square = jnp.mean(hidden_state * hidden_state, axis=-1, keepdims=True)
     normed = (hidden_state * lax.rsqrt(mean_square + 1e-06) * norm_gain.astype(jnp.float32)).astype(
         jnp.bfloat16
@@ -117,9 +125,14 @@
     shared_gate = jnp.dot(normed, sg_w, preferred_element_type=jnp.float32)
     shared_up = jnp.dot(normed, su_w, preferred_element_type=jnp.float32)
     shared_inner = (jax.nn.silu(shared_gate) * shared_up).astype(jnp.bfloat16)
-    inner_all = lax.all_gather(shared_inner, TP, axis=0)
-    shared_own = jnp.einsum(
-        "tqf,tsjf->qsj", inner_all, sd_own, preferred_element_type=jnp.float32
+    shared_own = sum(
+        jnp.einsum(
+            "qf,sjf->qsj",
+            b,
+            lax.dynamic_index_in_dim(sd_own, (tp_index - k) % n_tp, 0, keepdims=False),
+            preferred_element_type=jnp.float32,
+        )
+        for k, b in enumerate(tp_blocks(shared_inner, n_tp))
     ).reshape(tok_rows, width)
 
     flat_ids = expert_ids.reshape(tok_rows * TOPK)
@@ -135,22 +148,29 @@
     buffer = jnp.dot(dispatch, own_normed, preferred_element_type=jnp.float32).astype(jnp.bfloat16)
     buffer = buffer.reshape(expert_count, CAP, width)
     recv = lax.all_to_all(buffer, SEQ, split_axis=0, concat_axis=0, tiled=True)
-    rows_all = lax.all_gather(recv, TP, axis=0)
     ff = w_gate.shape[2]
-    gate_pre = jnp.einsum(
-        "tsrc,tcf->srf", rows_all, w_gate[0].reshape(n_tp, width, ff), preferred_element_type=jnp.float32
-    )
-    up_pre = jnp.einsum(
-        "tsrc,tcf->srf", rows_all, w_up[0].reshape(n_tp, width, ff), preferred_element_type=jnp.float32
-    )
+    rows_flat = recv.reshape(slots, width)
+    wg_b = w_gate[0].reshape(n_tp, width, ff)
+    wu_b = w_up[0].reshape(n_tp, width, ff)
+    wd_b = w_down[0].reshape(n_tp, ff, w_down.shape[2])
+    gate_pre = 0.0
+    up_pre = 0.0
+    for k, b in enumerate(tp_blocks(rows_flat, n_tp)):
+        src_tp = (tp_index - k) % n_tp
+        gate_pre = gate_pre + jnp.dot(
+            b, lax.dynamic_index_in_dim(wg_b, src_tp, 0, keepdims=False), preferred_element_type=jnp.float32
+        )
+        up_pre = up_pre + jnp.dot(
+            b, lax.dynamic_index_in_dim(wu_b, src_tp, 0, keepdims=False), preferred_element_type=jnp.float32
+        )
     inner = (jax.nn.silu(gate_pre) * up_pre).astype(jnp.bfloat16)
-    inner_r = lax.all_gather(inner, TP, axis=0)
-    out = jnp.einsum(
-        "tsrf,tfn->srn",
-        inner_r,
-        w_down[0].reshape(n_tp, ff, w_down.shape[2]),
-        preferred_element_type=jnp.float32,
-    ).astype(jnp.bfloat16)
+    out = 0.0
+    for k, b in enumerate(tp_blocks(inner, n_tp)):
+        src_tp = (tp_index - k) % n_tp
+        out = out + jnp.dot(
+            b, lax.dynamic_index_in_dim(wd_b, src_tp, 0, keepdims=False), preferred_element_type=jnp.float32
+        )
+    out = out.astype(jnp.bfloat16).reshape(expert_count, CAP, w_down.shape[2])
     returned = lax.all_to_all(out, SEQ, split_axis=0, concat_axis=0, tiled=True)
     picked_rows = returned.reshape(slots, width)[dest]
     weighted = picked_rows.astype(jnp.float32) * gates.reshape(tok_rows * TOPK)[:, None]

time: 580 us -> 500 us (0.86)
  starting transfers between devices: 17.1 us -> 175 us
  waiting for transfers between devices: 360 us -> 209 us
  blocking collectives: 129 us -> 28.1 us
  matrix products: 23.4 us -> 37.6 us
    all_gather x3 -> x0, waiting for transfers between devices: 258 us -> none  [the longest x1 112 us: local(): rows_all = lax.all_gather(recv, TP, axis=0)]
    ppermute x0 -> x35, starting transfers between devices: none -> 146 us  [tp_blocks(): out.append(lax.ppermute(x, TP, [(j, (j + k) % n_tp) for j in range(n_tp)]))]
    ppermute x0 -> x35, waiting for transfers between devices: none -> 90.2 us  [tp_blocks(): out.append(lax.ppermute(x, TP, [(j, (j + k) % n_tp) for j in range(n_tp)]))]
    all_gather x2 -> x0, blocking collectives: 60.3 us -> none  [the longest x1 35.2 us: local(): inner_all = lax.all_gather(shared_inner, TP, axis=0)]
    all_to_all x1 -> x0, blocking collectives: 38.4 us -> none  [local(): recv = lax.all_to_all(buffer, SEQ, split_axis=0, concat_axis=0, tiled=True)]
    all_to_all x1, waiting for transfers between devices: 19.1 us -> 0.01 us  [local(): sd_own = lax.all_to_all(sd_t, TP, split_axis=0, concat_axis=0, tiled=True)]
    all_gather x2, waiting for transfers between devices: 57.3 us -> 75.7 us  [gather_seq(): g = lax.all_gather(g, 'z', axis=0)]
    all_to_all x0 -> x1, starting transfers between devices: none -> 17.3 us  [local(): recv = lax.all_to_all(buffer, SEQ, split_axis=0, concat_axis=0, tiled=True)]
  transfers between devices with their start and end apart: 9 -> 42, of which waited for: 8 -> 16; matrix products, arithmetic and copies ran while one was open for 8% -> 13% of each run, Pallas kernels for 0% -> 0%
where the time goes in v2:
time: 500 us; the launch traced here: 497 us
  waiting for transfers between devices  209 us (42%)
  starting transfers between devices  175 us (35%)
  matrix products  37.6 us (8%)
  blocking collectives  28.1 us (6%)
  local copies, waits for them, and re-layouts  25.2 us (5%)
  between operations  14.6 us (3%)
  other arithmetic  7.01 us (1%)
    ppermute x35, starting transfers between devices, tp_blocks(): out.append(lax.ppermute(x, TP, [(j, (j + k) % n_tp) for j in range(n_tp)]))  146 us
    ppermute x35, waiting for transfers between devices, tp_blocks(): out.append(lax.ppermute(x, TP, [(j, (j + k) % n_tp) for j in range(n_tp)]))  90.2 us
    all_gather x2, waiting for transfers between devices, gather_seq(): g = lax.all_gather(g, 'z', axis=0)  75.7 us
    all_gather x2, blocking collectives, gather_seq(): g = lax.all_gather(x, 'yh', axis=0)  28.1 us
    all_gather x2, waiting for transfers between devices, gather_seq(): g = lax.all_gather(g, 'c', axis=0)  18.6 us
    all_to_all x1, starting transfers between devices, local(): recv = lax.all_to_all(buffer, SEQ, split_axis=0, concat_axis=0, tiled=True)  17.3 us
    all_to_all x1, waiting for transfers between devices, local(): returned = lax.all_to_all(out, SEQ, split_axis=0, concat_axis=0, tiled=True)  16.7 us
  transfers between devices with their start and end apart: 42, of which 16 were waited for; matrix products, arithmetic and copies ran while one was open for 13% of the time, Pallas kernels for 0%

profile of v2, /device:TPU:1, one launch (start us, length us, event | category | flops | bytes accessed | tf_op | source)
XLA Modules:
  0.0 497.1 jit_solution(17347083247937312451)
XLA Ops:
  7.4 15.5 %all-gather.3 = bf16[12,32,176]{2,1,0:T(8,128)(2,1)} all-gather(bf16[3,32,176]{2,1,0:T(8,128)(2,1)S(1)} %pad_maximum_fusion.1), channel_id=5, replica_groups=mesh['yh'=4,'z'=8,'c'=2,'x'=4,'yl'=2] {'yh'}, dimensions={0}, use_global_device_ids=true | all-gather | bytes 168960 | tf_op jit(solution)/shard_map/all_gather | solution.py:20
  23.7 12.6 %all-gather = bf16[1152,128]{1,0:T(8,128)(2,1)} all-gather(bf16[288,128]{1,0:T(8,128)(2,1)S(1)} %pad_maximum_fusion), channel_id=2, replica_groups=mesh['yh'=4,'z'=8,'c'=2,'x'=4,'yl'=2] {'yh'}, dimensions={0}, use_global_device_ids=true | all-gather | bytes 368640 | tf_op jit(solution)/shard_map/all_gather | solution.py:20
  36.4 31.1 %all-gather.15.cloned.1.call-done = bf16[32,3,32,176]{3,2,1,0:T(8,128)(2,1)} async-done(((bf16[4,3,32,176]{3,2,1,0:T(8,128)(2,1)}), bf16[32,3,32,176]{3,2,1,0:T(8,128)(2,1)}) %all-gather.15.cloned.1.call-update) | async-done | bytes 1081360 | tf_op jit(solution)/shard_map/all_gather | solution.py:21
  67.6 44.6 %all-gather.11.cloned.1.call-done = bf16[32,288,128]{2,1,0:T(8,128)(2,1)} async-done(((bf16[4,288,128]{2,1,0:T(8,128)(2,1)}), bf16[32,288,128]{2,1,0:T(8,128)(2,1)}) %all-gather.11.cloned.1.call-update) | async-done | bytes 2359312 | tf_op jit(solution)/shard_map/all_gather | solution.py:21
  112.2 3.2 collective-permute-start.1
  115.5 4.0 collective-permute-start.5
  119.5 3.4 collective-permute-start.7
  122.9 4.9 collective-permute-start.9
  133.1 4.4 constant_dynamic-slice_fusion.5
  138.3 2.3 copy.61
  142.4 3.9 all-to-all-start
  146.3 17.9 %all-gather.13.cloned.1.call-done = bf16[16,4,288,128]{3,2,1,0:T(8,128)(2,1)} async-done(((bf16[8,4,288,128]{3,2,1,0:T(8,128)(2,1)}), bf16[16,4,288,128]{3,2,1,0:T(8,128)(2,1)}) %all-gather.13.cloned.1.call-update) | async-done | bytes 4718608 | tf_op jit(solution)/shard_map/all_gather | solution.py:22
  164.2 2.7 fusion.173
  175.7 4.3 collective-permute-start.11
  183.5 4.2 collective-permute-start.13
  187.7 3.4 collective-permute-start.6
  192.5 2.8 collective-permute-start.3
  195.3 3.2 collective-permute-start.8
  199.8 12.9 %collective-permute-start.10 = (bf16[128,128]{1,0:T(8,128)(2,1)S(1)}, bf16[128,128]{1,0:T(8,128)(2,1)S(1)}, u32[]{:S(2)}, u32[]{:S(2)}) collective-permute-start(bf16[128,128]{1,0:T(8,128)(2,1)S(1)} %fusion.34), channel_id=1, source_target_pairs={{0,6},{1,7},{2,0},{3,1},{4,2},{5,3},{6,4},{7,5},{8,14},{9,15},{10,... | collective-permute-start | bytes 98312 | tf_op jit(solution)/shard_map/ppermute | solution.py:29
  218.6 3.3 collective-permute-done.2
  227.8 17.3 %all-to-all-start.1 = ((bf16[64,18,256]{2,1,0:T(8,128)(2,1)}), bf16[64,18,256]{2,1,0:T(8,128)(2,1)}, u32[]{:S(2)}, u32[]{:S(2)}) async-start(bf16[64,18,256]{2,1,0:T(8,128)(2,1)} %reshape.318), calls=%async_computation.1 | async-start | bytes 1572864 | tf_op jit(solution)/shard_map/all_to_all | solution.py:150
  245.1 2.3 fusion.33
  247.4 2.7 collective-permute-start.14
  250.1 4.7 collective-permute-start.20
  261.7 8.1 %all-to-all-done.1 = bf16[64,18,256]{2,1,0:T(8,128)(2,1)} async-done(((bf16[64,18,256]{2,1,0:T(8,128)(2,1)}), bf16[64,18,256]{2,1,0:T(8,128)(2,1)}, u32[]{:S(2)}, u32[]{:S(2)}) %all-to-all-start.1) | async-done | bytes 589856 | tf_op jit(solution)/shard_map/all_to_all | solution.py:150
  274.8 2.4 collective-permute-start.26
  279.9 8.2 %collective-permute-done.27 = bf16[1152,256]{1,0:T(8,128)(2,1)S(1)} collective-permute-done((bf16[1152,256]{1,0:T(8,128)(2,1)S(1)}, bf16[1152,256]{1,0:T(8,128)(2,1)S(1)}, u32[]{:S(2)}, u32[]{:S(2)}) %collective-permute-start.27) | collective-permute-done | bytes 589856 | tf_op jit(solution)/shard_map/ppermute | solution.py:29
  288.0 2.7 collective-permute-start.25
  291.5 4.7 collective-permute-start.24
  297.0 7.9 %collective-permute-done.25 = bf16[1152,256]{1,0:T(8,128)(2,1)S(1)} collective-permute-done((bf16[1152,256]{1,0:T(8,128)(2,1)S(1)}, bf16[1152,256]{1,0:T(8,128)(2,1)S(1)}, u32[]{:S(2)}, u32[]{:S(2)}) %collective-permute-start.25) | collective-permute-done | bytes 589856 | tf_op jit(solution)/shard_map/ppermute | solution.py:29
  304.9 16.1 %collective-permute-start.23 = (bf16[1152,256]{1,0:T(8,128)(2,1)S(1)}, bf16[1152,256]{1,0:T(8,128)(2,1)S(1)}, u32[]{:S(2)}, u32[]{:S(2)}) collective-permute-start(bf16[1152,256]{1,0:T(8,128)(2,1)S(1)} %reshape.319), channel_id=1, source_target_pairs={{0,3},{1,4},{2,5},{3,6},{4,7},{5,0},{6,1},{7,2},{8,11},{9,12},{10,... | collective-permute-start | bytes 1769480 | tf_op jit(solution)/shard_map/ppermute | solution.py:29
  321.8 26.0 %collective-permute-start.21 = (bf16[1152,256]{1,0:T(8,128)(2,1)S(1)}, bf16[1152,256]{1,0:T(8,128)(2,1)S(1)}, u32[]{:S(2)}, u32[]{:S(2)}) collective-permute-start(bf16[1152,256]{1,0:T(8,128)(2,1)S(1)} %reshape.319), channel_id=1, source_target_pairs={{0,1},{1,2},{2,3},{3,4},{4,5},{5,6},{6,7},{7,0},{8,9},{9,10},{10,1... | collective-permute-start | bytes 1769480 | tf_op jit(solution)/shard_map/ppermute | solution.py:29
  351.2 7.9 %collective-permute-done.21 = bf16[1152,256]{1,0:T(8,128)(2,1)S(1)} collective-permute-done((bf16[1152,256]{1,0:T(8,128)(2,1)S(1)}, bf16[1152,256]{1,0:T(8,128)(2,1)S(1)}, u32[]{:S(2)}, u32[]{:S(2)}) %collective-permute-start.21) | collective-permute-done | bytes 589856 | tf_op jit(solution)/shard_map/ppermute | solution.py:29
  359.1 2.7 collective-permute-start.17
  362.6 10.6 %collective-permute-done.22 = bf16[1152,256]{1,0:T(8,128)(2,1)S(1)} collective-permute-done((bf16[1152,256]{1,0:T(8,128)(2,1)S(1)}, bf16[1152,256]{1,0:T(8,128)(2,1)S(1)}, u32[]{:S(2)}, u32[]{:S(2)}) %collective-permute-start.22) | collective-permute-done | bytes 589856 | tf_op jit(solution)/shard_map/ppermute | solution.py:29
  374.8 3.5 collective-permute-start.33
  381.6 15.1 %collective-permute-done.33 = bf16[1152,176]{0,1:T(8,128)(2,1)S(1)} collective-permute-done((bf16[1152,176]{0,1:T(8,128)(2,1)S(1)}, bf16[1152,176]{0,1:T(8,128)(2,1)S(1)}, u32[]{:S(2)}, u32[]{:S(2)}) %collective-permute-start.33) | collective-permute-done | bytes 405536 | tf_op jit(solution)/shard_map/ppermute | solution.py:29
  396.7 2.7 collective-permute-start.31
  399.8 2.1 collective-permute-start.30
  402.3 16.3 %collective-permute-done.31 = bf16[1152,176]{0,1:T(8,128)(2,1)S(1)} collective-permute-done((bf16[1152,176]{0,1:T(8,128)(2,1)S(1)}, bf16[1152,176]{0,1:T(8,128)(2,1)S(1)}, u32[]{:S(2)}, u32[]{:S(2)}) %collective-permute-start.31) | collective-permute-done | bytes 405536 | tf_op jit(solution)/shard_map/ppermute | solution.py:29
  420.9 3.4 collective-permute-start.28
  424.6 4.7 collective-permute-done.34
  429.4 2.5 collective-permute-start.29
  432.3 6.8 %collective-permute-done.28 = bf16[1152,176]{0,1:T(8,128)(2,1)S(1)} collective-permute-done((bf16[1152,176]{0,1:T(8,128)(2,1)S(1)}, bf16[1152,176]{0,1:T(8,128)(2,1)S(1)}, u32[]{:S(2)}, u32[]{:S(2)}) %collective-permute-start.28) | collective-permute-done | bytes 405536 | tf_op jit(solution)/shard_map/ppermute | solution.py:29
  441.4 9.3 %collective-permute-done.29 = bf16[1152,176]{0,1:T(8,128)(2,1)S(1)} collective-permute-done((bf16[1152,176]{0,1:T(8,128)(2,1)S(1)}, bf16[1152,176]{0,1:T(8,128)(2,1)S(1)}, u32[]{:S(2)}, u32[]{:S(2)}) %collective-permute-start.29) | collective-permute-done | bytes 405536 | tf_op jit(solution)/shard_map/ppermute | solution.py:29
  454.2 7.8 %all-to-all-start.2 = ((bf16[64,18,256]{2,1,0:T(8,128)(2,1)}), bf16[64,18,256]{2,1,0:T(8,128)(2,1)}, u32[]{:S(2)}, u32[]{:S(2)}) async-start(bf16[64,18,256]{2,1,0:T(8,128)(2,1)} %reshape.320), calls=%async_computation.2 | async-start | bytes 1572864 | tf_op jit(solution)/shard_map/all_to_all | solution.py:174
  468.8 16.7 %all-to-all-done.2 = bf16[64,18,256]{2,1,0:T(8,128)(2,1)} async-done(((bf16[64,18,256]{2,1,0:T(8,128)(2,1)}), bf16[64,18,256]{2,1,0:T(8,128)(2,1)}, u32[]{:S(2)}, u32[]{:S(2)}) %all-to-all-start.2) | async-done | bytes 589856 | tf_op jit(solution)/shard_map/all_to_all | solution.py:174
  486.8 2.7 gather_fusion.1
  (189 shorter events, 79.9 us)
Async XLA Ops:
  6.5 374.7 %copy-start = (bf16[1,1408,256]{2,1,0:T(8,128)(2,1)S(1)}, bf16[1,1408,256]{2,1,0:T(8,128)(2,1)}, u32[]{:S(2)}) copy-start(bf16[1,1408,256]{2,1,0:T(8,128)(2,1)} %param.30) | copy-start | bytes 2162692
  6.5 61.0 %all-gather.15.cloned.1.call-start = ((), (), s32[]{:S(2)}) async-start(), calls=%async_computation.5 | async-start | bytes 1769472 | tf_op jit(solution)/shard_map/all_gather | solution.py:21
  22.9 89.3 %all-gather.11.cloned.1.call-start = ((), (), s32[]{:S(2)}) async-start(), calls=%async_computation.3 | async-start | bytes 2654208 | tf_op jit(solution)/shard_map/all_gather | solution.py:21
  36.3 91.6 %copy-start.21 = (s32[128,6]{0,1:T(8,128)S(1)}, s32[128,6]{0,1:T(8,128)}, u32[]{:S(2)}) copy-start(s32[128,6]{0,1:T(8,128)} %param.27) | copy-start | bytes 9220
  36.3 102.0 %all-gather.17.cloned.1.call-start = ((), (), s32[]{:S(2)}) async-start(), calls=%async_computation.6 | async-start | bytes 4718592 | tf_op jit(solution)/shard_map/all_gather | solution.py:22
  67.5 60.9 %copy-start.1 = (s32[64]{0:T(128)S(1)}, s32[64]{0:T(128)}, u32[]{:S(2)}) copy-start(s32[64]{0:T(128)} %param.23) | copy-start | bytes 772
  67.5 61.9 %copy-start.22 = (bf16[2048]{0:T(1024)(128)(2,1)S(1)}, bf16[2048]{0:T(1024)(128)(2,1)}, u32[]{:S(2)}) copy-start(bf16[2048]{0:T(1024)(128)(2,1)} %param.25) | copy-start | bytes 12292
  67.5 96.6 %all-gather.13.cloned.1.call-start = ((), (), s32[]{:S(2)}) async-start(), calls=%async_computation.4 | async-start | bytes 7077888 | tf_op jit(solution)/shard_map/all_gather | solution.py:22
  112.2 63.5 %collective-permute-start.1 = (bf16[128,2048]{1,0:T(8,128)(2,1)}, bf16[128,2048]{1,0:T(8,128)(2,1)}, u32[]{:S(2)}, u32[]{:S(2)}) collective-permute-start(bf16[128,2048]{1,0:T(8,128)(2,1)} %param.24), channel_id=1, source_target_pairs={{0,1},{1,2},{2,3},{3,4},{4,5},{5,6},{6,7},{7,0},{8,9},{9,10},{10,1... | collective-permute-start | bytes 1572872 | tf_op jit(solution)/shard_map/ppermute | solution.py:29
  115.5 68.0 %collective-permute-start.5 = (bf16[128,2048]{1,0:T(8,128)(2,1)}, bf16[128,2048]{1,0:T(8,128)(2,1)}, u32[]{:S(2)}, u32[]{:S(2)}) collective-permute-start(bf16[128,2048]{1,0:T(8,128)(2,1)} %param.24), channel_id=1, source_target_pairs={{0,3},{1,4},{2,5},{3,6},{4,7},{5,0},{6,1},{7,2},{8,11},{9,12},{10,... | collective-permute-start | bytes 1572872 | tf_op jit(solution)/shard_map/ppermute | solution.py:29
  119.5 73.0 %collective-permute-start.7 = (bf16[128,2048]{1,0:T(8,128)(2,1)}, bf16[128,2048]{1,0:T(8,128)(2,1)}, u32[]{:S(2)}, u32[]{:S(2)}) collective-permute-start(bf16[128,2048]{1,0:T(8,128)(2,1)} %param.24), channel_id=1, source_target_pairs={{0,4},{1,5},{2,6},{3,7},{4,0},{5,1},{6,2},{7,3},{8,12},{9,13},{10,... | collective-permute-start | bytes 1572872 | tf_op jit(solution)/shard_map/ppermute | solution.py:29
  122.9 77.0 %collective-permute-start.9 = (bf16[128,2048]{1,0:T(8,128)(2,1)}, bf16[128,2048]{1,0:T(8,128)(2,1)}, u32[]{:S(2)}, u32[]{:S(2)}) collective-permute-start(bf16[128,2048]{1,0:T(8,128)(2,1)} %param.24), channel_id=1, source_target_pairs={{0,5},{1,6},{2,7},{3,0},{4,1},{5,2},{6,3},{7,4},{8,13},{9,14},{10,... | collective-permute-start | bytes 1572872 | tf_op jit(solution)/shard_map/ppermute | solution.py:29
  142.4 85.4 %all-to-all-start = ((bf16[8,8,32,176]{3,2,1,0:T(8,128)(2,1)}), bf16[8,8,32,176]{3,2,1,0:T(8,128)(2,1)S(1)}, u32[]{:S(2)}, u32[]{:S(2)}) async-start(bf16[8,8,32,176]{3,2,1,0:T(8,128)(2,1)} %bitcast.22), calls=%async_computation | async-start | bytes 2097152 | tf_op jit(solution)/shard_map/all_to_all | solution.py:69
  172.2 7.8 %collective-permute-start = (bf16[128,128]{1,0:T(8,128)(2,1)S(1)}, bf16[128,128]{1,0:T(8,128)(2,1)S(1)}, u32[]{:S(2)}, u32[]{:S(2)}) collective-permute-start(bf16[128,128]{1,0:T(8,128)(2,1)S(1)} %fusion.34), channel_id=1, source_target_pairs={{0,1},{1,2},{2,3},{3,4},{4,5},{5,6},{6,7},{7,0},{8,9},{9,10},{10,1... | collective-permute-start | bytes 98312 | tf_op jit(solution)/shard_map/ppermute | solution.py:29
  175.7 40.4 %collective-permute-start.11 = (bf16[128,2048]{1,0:T(8,128)(2,1)}, bf16[128,2048]{1,0:T(8,128)(2,1)S(1)}, u32[]{:S(2)}, u32[]{:S(2)}) collective-permute-start(bf16[128,2048]{1,0:T(8,128)(2,1)} %param.24), channel_id=1, source_target_pairs={{0,6},{1,7},{2,0},{3,1},{4,2},{5,3},{6,4},{7,5},{8,14},{9,15},{10,... | collective-permute-start | bytes 1572872 | tf_op jit(solution)/shard_map/ppermute | solution.py:29
  180.0 7.7 %collective-permute-start.4 = (bf16[128,128]{1,0:T(8,128)(2,1)S(1)}, bf16[128,128]{1,0:T(8,128)(2,1)S(1)}, u32[]{:S(2)}, u32[]{:S(2)}) collective-permute-start(bf16[128,128]{1,0:T(8,128)(2,1)S(1)} %fusion.34), channel_id=1, source_target_pairs={{0,3},{1,4},{2,5},{3,6},{4,7},{5,0},{6,1},{7,2},{8,11},{9,12},{10,... | collective-permute-start | bytes 98312 | tf_op jit(solution)/shard_map/ppermute | solution.py:29
  183.5 34.8 %collective-permute-start.13 = (bf16[128,2048]{1,0:T(8,128)(2,1)}, bf16[128,2048]{1,0:T(8,128)(2,1)S(1)}, u32[]{:S(2)}, u32[]{:S(2)}) collective-permute-start(bf16[128,2048]{1,0:T(8,128)(2,1)} %param.24), channel_id=1, source_target_pairs={{0,7},{1,0},{2,1},{3,2},{4,3},{5,4},{6,5},{7,6},{8,15},{9,8},{10,9... | collective-permute-start | bytes 1572872 | tf_op jit(solution)/shard_map/ppermute | solution.py:29
  187.7 7.6 %collective-permute-start.6 = (bf16[128,128]{1,0:T(8,128)(2,1)S(1)}, bf16[128,128]{1,0:T(8,128)(2,1)S(1)}, u32[]{:S(2)}, u32[]{:S(2)}) collective-permute-start(bf16[128,128]{1,0:T(8,128)(2,1)S(1)} %fusion.34), channel_id=1, source_target_pairs={{0,4},{1,5},{2,6},{3,7},{4,0},{5,1},{6,2},{7,3},{8,12},{9,13},{10,... | collective-permute-start | bytes 98312 | tf_op jit(solution)/shard_map/ppermute | solution.py:29
  192.5 26.1 %collective-permute-start.3 = (bf16[128,2048]{1,0:T(8,128)(2,1)}, bf16[128,2048]{1,0:T(8,128)(2,1)S(1)}, u32[]{:S(2)}, u32[]{:S(2)}) collective-permute-start(bf16[128,2048]{1,0:T(8,128)(2,1)} %param.24), channel_id=1, source_target_pairs={{0,2},{1,3},{2,4},{3,5},{4,6},{5,7},{6,0},{7,1},{8,10},{9,11},{10,... | collective-permute-start | bytes 1572872 | tf_op jit(solution)/shard_map/ppermute | solution.py:29
  195.3 17.5 %collective-permute-start.8 = (bf16[128,128]{1,0:T(8,128)(2,1)S(1)}, bf16[128,128]{1,0:T(8,128)(2,1)S(1)}, u32[]{:S(2)}, u32[]{:S(2)}) collective-permute-start(bf16[128,128]{1,0:T(8,128)(2,1)S(1)} %fusion.34), channel_id=1, source_target_pairs={{0,5},{1,6},{2,7},{3,0},{4,1},{5,2},{6,3},{7,4},{8,13},{9,14},{10,... | collective-permute-start | bytes 98312 | tf_op jit(solution)/shard_map/ppermute | solution.py:29
  199.8 18.2 %collective-permute-start.10 = (bf16[128,128]{1,0:T(8,128)(2,1)S(1)}, bf16[128,128]{1,0:T(8,128)(2,1)S(1)}, u32[]{:S(2)}, u32[]{:S(2)}) collective-permute-start(bf16[128,128]{1,0:T(8,128)(2,1)S(1)} %fusion.34), channel_id=1, source_target_pairs={{0,6},{1,7},{2,0},{3,1},{4,2},{5,3},{6,4},{7,5},{8,14},{9,15},{10,... | collective-permute-start | bytes 98312 | tf_op jit(solution)/shard_map/ppermute | solution.py:29
  212.8 5.5 %collective-permute-start.12 = (bf16[128,128]{1,0:T(8,128)(2,1)S(1)}, bf16[128,128]{1,0:T(8,128)(2,1)S(1)}, u32[]{:S(2)}, u32[]{:S(2)}) collective-permute-start(bf16[128,128]{1,0:T(8,128)(2,1)S(1)} %fusion.34), channel_id=1, source_target_pairs={{0,7},{1,0},{2,1},{3,2},{4,3},{5,4},{6,5},{7,6},{8,15},{9,8},{10,9... | collective-permute-start | bytes 98312 | tf_op jit(solution)/shard_map/ppermute | solution.py:29
  216.1 5.9 %collective-permute-start.2 = (bf16[128,128]{1,0:T(8,128)(2,1)S(1)}, bf16[128,128]{1,0:T(8,128)(2,1)S(1)}, u32[]{:S(2)}, u32[]{:S(2)}) collective-permute-start(bf16[128,128]{1,0:T(8,128)(2,1)S(1)} %fusion.34), channel_id=1, source_target_pairs={{0,2},{1,3},{2,4},{3,5},{4,6},{5,7},{6,0},{7,1},{8,10},{9,11},{10,... | collective-permute-start | bytes 98312 | tf_op jit(solution)/shard_map/ppermute | solution.py:29
  227.8 42.0 %all-to-all-start.1 = ((bf16[64,18,256]{2,1,0:T(8,128)(2,1)}), bf16[64,18,256]{2,1,0:T(8,128)(2,1)}, u32[]{:S(2)}, u32[]{:S(2)}) async-start(bf16[64,18,256]{2,1,0:T(8,128)(2,1)} %reshape.318), calls=%async_computation.1 | async-start | bytes 1572864 | tf_op jit(solution)/shard_map/all_to_all | solution.py:150
  247.4 25.8 %collective-permute-start.14 = (bf16[128,176]{0,1:T(8,128)(2,1)}, bf16[128,176]{0,1:T(8,128)(2,1)}, u32[]{:S(2)}, u32[]{:S(2)}) collective-permute-start(bf16[128,176]{0,1:T(8,128)(2,1)} %fusion.33), channel_id=1, source_target_pairs={{0,1},{1,2},{2,3},{3,4},{4,5},{5,6},{6,7},{7,0},{8,9},{9,10},{10,1... | collective-permute-start | bytes 135176 | tf_op jit(solution)/shard_map/ppermute | solution.py:29
  250.1 128.2 %collective-permute-start.20 = (bf16[128,176]{0,1:T(8,128)(2,1)}, bf16[128,176]{0,1:T(8,128)(2,1)}, u32[]{:S(2)}, u32[]{:S(2)}) collective-permute-start(bf16[128,176]{0,1:T(8,128)(2,1)} %fusion.33), channel_id=1, source_target_pairs={{0,7},{1,0},{2,1},{3,2},{4,3},{5,4},{6,5},{7,6},{8,15},{9,8},{10,9... | collective-permute-start | bytes 135176 | tf_op jit(solution)/shard_map/ppermute | solution.py:29
  254.8 207.3 %collective-permute-start.19 = (bf16[128,176]{0,1:T(8,128)(2,1)}, bf16[128,176]{0,1:T(8,128)(2,1)}, u32[]{:S(2)}, u32[]{:S(2)}) collective-permute-start(bf16[128,176]{0,1:T(8,128)(2,1)} %fusion.33), channel_id=1, source_target_pairs={{0,6},{1,7},{2,0},{3,1},{4,2},{5,3},{6,4},{7,5},{8,14},{9,15},{10,... | collective-permute-start | bytes 135176 | tf_op jit(solution)/shard_map/ppermute | solution.py:29
  256.7 206.3 %collective-permute-start.18 = (bf16[128,176]{0,1:T(8,128)(2,1)}, bf16[128,176]{0,1:T(8,128)(2,1)}, u32[]{:S(2)}, u32[]{:S(2)}) collective-permute-start(bf16[128,176]{0,1:T(8,128)(2,1)} %fusion.33), channel_id=1, source_target_pairs={{0,5},{1,6},{2,7},{3,0},{4,1},{5,2},{6,3},{7,4},{8,13},{9,14},{10,... | collective-permute-start | bytes 135176 | tf_op jit(solution)/shard_map/ppermute | solution.py:29
  271.1 16.9 %collective-permute-start.27 = (bf16[1152,256]{1,0:T(8,128)(2,1)S(1)}, bf16[1152,256]{1,0:T(8,128)(2,1)S(1)}, u32[]{:S(2)}, u32[]{:S(2)}) collective-permute-start(bf16[1152,256]{1,0:T(8,128)(2,1)S(1)} %reshape.319), channel_id=1, source_target_pairs={{0,7},{1,0},{2,1},{3,2},{4,3},{5,4},{6,5},{7,6},{8,15},{9,8},{10,9... | collective-permute-start | bytes 1769480 | tf_op jit(solution)/shard_map/ppermute | solution.py:29
  274.8 16.7 %collective-permute-start.26 = (bf16[1152,256]{1,0:T(8,128)(2,1)S(1)}, bf16[1152,256]{1,0:T(8,128)(2,1)S(1)}, u32[]{:S(2)}, u32[]{:S(2)}) collective-permute-start(bf16[1152,256]{1,0:T(8,128)(2,1)S(1)} %reshape.319), channel_id=1, source_target_pairs={{0,6},{1,7},{2,0},{3,1},{4,2},{5,3},{6,4},{7,5},{8,14},{9,15},{10,... | collective-permute-start | bytes 1769480 | tf_op jit(solution)/shard_map/ppermute | solution.py:29
  288.0 16.8 %collective-permute-start.25 = (bf16[1152,256]{1,0:T(8,128)(2,1)S(1)}, bf16[1152,256]{1,0:T(8,128)(2,1)S(1)}, u32[]{:S(2)}, u32[]{:S(2)}) collective-permute-start(bf16[1152,256]{1,0:T(8,128)(2,1)S(1)} %reshape.319), channel_id=1, source_target_pairs={{0,5},{1,6},{2,7},{3,0},{4,1},{5,2},{6,3},{7,4},{8,13},{9,14},{10,... | collective-permute-start | bytes 1769480 | tf_op jit(solution)/shard_map/ppermute | solution.py:29
  291.1 29.9 %copy-start.12 = (bf16[1,256,176]{1,0,2:T(2,128)(2,1)S(1)}, bf16[1,256,176]{1,0,2:T(2,128)(2,1)}, u32[]{:S(2)}) copy-start(bf16[1,256,176]{1,0,2:T(2,128)(2,1)} %get-tuple-element.40) | copy-start | bytes 270340
  291.5 30.3 %collective-permute-start.24 = (bf16[1152,256]{1,0:T(8,128)(2,1)S(1)}, bf16[1152,256]{1,0:T(8,128)(2,1)S(1)}, u32[]{:S(2)}, u32[]{:S(2)}) collective-permute-start(bf16[1152,256]{1,0:T(8,128)(2,1)S(1)} %reshape.319), channel_id=1, source_target_pairs={{0,4},{1,5},{2,6},{3,7},{4,0},{5,1},{6,2},{7,3},{8,12},{9,13},{10,... | collective-permute-start | bytes 1769480 | tf_op jit(solution)/shard_map/ppermute | solution.py:29
  296.6 51.2 %copy-start.10 = (bf16[1,256,176]{1,0,2:T(2,128)(2,1)S(1)}, bf16[1,256,176]{1,0,2:T(2,128)(2,1)}, u32[]{:S(2)}) copy-start(bf16[1,256,176]{1,0,2:T(2,128)(2,1)} %get-tuple-element.39) | copy-start | bytes 270340
  304.9 43.7 %collective-permute-start.23 = (bf16[1152,256]{1,0:T(8,128)(2,1)S(1)}, bf16[1152,256]{1,0:T(8,128)(2,1)S(1)}, u32[]{:S(2)}, u32[]{:S(2)}) collective-permute-start(bf16[1152,256]{1,0:T(8,128)(2,1)S(1)} %reshape.319), channel_id=1, source_target_pairs={{0,3},{1,4},{2,5},{3,6},{4,7},{5,0},{6,1},{7,2},{8,11},{9,12},{10,... | collective-permute-start | bytes 1769480 | tf_op jit(solution)/shard_map/ppermute | solution.py:29
  321.8 37.4 %collective-permute-start.21 = (bf16[1152,256]{1,0:T(8,128)(2,1)S(1)}, bf16[1152,256]{1,0:T(8,128)(2,1)S(1)}, u32[]{:S(2)}, u32[]{:S(2)}) collective-permute-start(bf16[1152,256]{1,0:T(8,128)(2,1)S(1)} %reshape.319), channel_id=1, source_target_pairs={{0,1},{1,2},{2,3},{3,4},{4,5},{5,6},{6,7},{7,0},{8,9},{9,10},{10,1... | collective-permute-start | bytes 1769480 | tf_op jit(solution)/shard_map/ppermute | solution.py:29
  348.6 24.6 %collective-permute-start.22 = (bf16[1152,256]{1,0:T(8,128)(2,1)S(1)}, bf16[1152,256]{1,0:T(8,128)(2,1)S(1)}, u32[]{:S(2)}, u32[]{:S(2)}) collective-permute-start(bf16[1152,256]{1,0:T(8,128)(2,1)S(1)} %reshape.319), channel_id=1, source_target_pairs={{0,2},{1,3},{2,4},{3,5},{4,6},{5,7},{6,0},{7,1},{8,10},{9,11},{10,... | collective-permute-start | bytes 1769480 | tf_op jit(solution)/shard_map/ppermute | solution.py:29
  359.1 104.9 %collective-permute-start.17 = (bf16[128,176]{0,1:T(8,128)(2,1)}, bf16[128,176]{0,1:T(8,128)(2,1)}, u32[]{:S(2)}, u32[]{:S(2)}) collective-permute-start(bf16[128,176]{0,1:T(8,128)(2,1)} %fusion.33), channel_id=1, source_target_pairs={{0,4},{1,5},{2,6},{3,7},{4,0},{5,1},{6,2},{7,3},{8,12},{9,13},{10,... | collective-permute-start | bytes 135176 | tf_op jit(solution)/shard_map/ppermute | solution.py:29
  374.8 22.0 %collective-permute-start.33 = (bf16[1152,176]{0,1:T(8,128)(2,1)S(1)}, bf16[1152,176]{0,1:T(8,128)(2,1)S(1)}, u32[]{:S(2)}, u32[]{:S(2)}) collective-permute-start(bf16[1152,176]{0,1:T(8,128)(2,1)S(1)} %multiply_convert_fusion.1), channel_id=1, source_target_pairs={{0,6},{1,7},{2,0},{3,1},{4,2},{5,3},{6,4},{7,5},{8,14},{9,15},{10,... | collective-permute-start | bytes 1216520 | tf_op jit(solution)/shard_map/ppermute | solution.py:29
  379.3 20.5 %collective-permute-start.32 = (bf16[1152,176]{0,1:T(8,128)(2,1)S(1)}, bf16[1152,176]{0,1:T(8,128)(2,1)S(1)}, u32[]{:S(2)}, u32[]{:S(2)}) collective-permute-start(bf16[1152,176]{0,1:T(8,128)(2,1)S(1)} %multiply_convert_fusion.1), channel_id=1, source_target_pairs={{0,5},{1,6},{2,7},{3,0},{4,1},{5,2},{6,3},{7,4},{8,13},{9,14},{10,... | collective-permute-start | bytes 1216520 | tf_op jit(solution)/shard_map/ppermute | solution.py:29
  396.7 21.8 %collective-permute-start.31 = (bf16[1152,176]{0,1:T(8,128)(2,1)S(1)}, bf16[1152,176]{0,1:T(8,128)(2,1)S(1)}, u32[]{:S(2)}, u32[]{:S(2)}) collective-permute-start(bf16[1152,176]{0,1:T(8,128)(2,1)S(1)} %multiply_convert_fusion.1), channel_id=1, source_target_pairs={{0,4},{1,5},{2,6},{3,7},{4,0},{5,1},{6,2},{7,3},{8,12},{9,13},{10,... | collective-permute-start | bytes 1216520 | tf_op jit(solution)/shard_map/ppermute | solution.py:29
  399.8 21.1 %collective-permute-start.30 = (bf16[1152,176]{0,1:T(8,128)(2,1)S(1)}, bf16[1152,176]{0,1:T(8,128)(2,1)S(1)}, u32[]{:S(2)}, u32[]{:S(2)}) collective-permute-start(bf16[1152,176]{0,1:T(8,128)(2,1)S(1)} %multiply_convert_fusion.1), channel_id=1, source_target_pairs={{0,3},{1,4},{2,5},{3,6},{4,7},{5,0},{6,1},{7,2},{8,11},{9,12},{10,... | collective-permute-start | bytes 1216520 | tf_op jit(solution)/shard_map/ppermute | solution.py:29
  418.6 10.8 %collective-permute-start.34 = (bf16[1152,176]{0,1:T(8,128)(2,1)S(1)}, bf16[1152,176]{0,1:T(8,128)(2,1)S(1)}, u32[]{:S(2)}, u32[]{:S(2)}) collective-permute-start(bf16[1152,176]{0,1:T(8,128)(2,1)S(1)} %multiply_convert_fusion.1), channel_id=1, source_target_pairs={{0,7},{1,0},{2,1},{3,2},{4,3},{5,4},{6,5},{7,6},{8,15},{9,8},{10,9... | collective-permute-start | bytes 1216520 | tf_op jit(solution)/shard_map/ppermute | solution.py:29
  420.9 18.2 %collective-permute-start.28 = (bf16[1152,176]{0,1:T(8,128)(2,1)S(1)}, bf16[1152,176]{0,1:T(8,128)(2,1)S(1)}, u32[]{:S(2)}, u32[]{:S(2)}) collective-permute-start(bf16[1152,176]{0,1:T(8,128)(2,1)S(1)} %multiply_convert_fusion.1), channel_id=1, source_target_pairs={{0,1},{1,2},{2,3},{3,4},{4,5},{5,6},{6,7},{7,0},{8,9},{9,10},{10,1... | collective-permute-start | bytes 1216520 | tf_op jit(solution)/shard_map/ppermute | solution.py:29
  429.4 21.3 %collective-permute-start.29 = (bf16[1152,176]{0,1:T(8,128)(2,1)S(1)}, bf16[1152,176]{0,1:T(8,128)(2,1)S(1)}, u32[]{:S(2)}, u32[]{:S(2)}) collective-permute-start(bf16[1152,176]{0,1:T(8,128)(2,1)S(1)} %multiply_convert_fusion.1), channel_id=1, source_target_pairs={{0,2},{1,3},{2,4},{3,5},{4,6},{5,7},{6,0},{7,1},{8,10},{9,11},{10,... | collective-permute-start | bytes 1216520 | tf_op jit(solution)/shard_map/ppermute | solution.py:29
  439.1 25.9 %collective-permute-start.16 = (bf16[128,176]{0,1:T(8,128)(2,1)}, bf16[128,176]{0,1:T(8,128)(2,1)}, u32[]{:S(2)}, u32[]{:S(2)}) collective-permute-start(bf16[128,176]{0,1:T(8,128)(2,1)} %fusion.33), channel_id=1, source_target_pairs={{0,3},{1,4},{2,5},{3,6},{4,7},{5,0},{6,1},{7,2},{8,11},{9,12},{10,... | collective-permute-start | bytes 135176 | tf_op jit(solution)/shard_map/ppermute | solution.py:29
  450.7 15.3 %collective-permute-start.15 = (bf16[128,176]{0,1:T(8,128)(2,1)}, bf16[128,176]{0,1:T(8,128)(2,1)}, u32[]{:S(2)}, u32[]{:S(2)}) collective-permute-start(bf16[128,176]{0,1:T(8,128)(2,1)} %fusion.33), channel_id=1, source_target_pairs={{0,2},{1,3},{2,4},{3,5},{4,6},{5,7},{6,0},{7,1},{8,10},{9,11},{10,... | collective-permute-start | bytes 135176 | tf_op jit(solution)/shard_map/ppermute | solution.py:29
  454.2 31.2 %all-to-all-start.2 = ((bf16[64,18,256]{2,1,0:T(8,128)(2,1)}), bf16[64,18,256]{2,1,0:T(8,128)(2,1)}, u32[]{:S(2)}, u32[]{:S(2)}) async-start(bf16[64,18,256]{2,1,0:T(8,128)(2,1)} %reshape.320), calls=%async_computation.2 | async-start | bytes 1572864 | tf_op jit(solution)/shard_map/all_to_all | solution.py:174
  (17 other events, 247.2 us)
Sparse Core Ops, SparseCore 0:
  23.0 44.4 all-gather.14
  69.6 42.5 all-gather.10
  114.3 23.9 all-gather.16
  140.2 23.8 all-gather.12
